TPU v7x, 128 devices: a whole 4x4x4 slice. The times are simulated.
128 devices in a mesh: rep: 16 (over y_hi, x, core), shard: 8 (over z, y_lo).
Axes of the slice: x: 4, y: 4 (y_hi: 2, y_lo: 2; y = y_hi * 2 + y_lo), z: 4, core: 2. Of those that a mesh axis runs over, the one named last changes fastest.
Arguments:
- layer_in: float32 [32768, 1024], P(('rep', 'shard')), may hold values from -6 to 6
- cotangent: float32 [32768, 1024], P(('rep', 'shard')), may hold values from -6 to 6
- seq_lengths: int32 [128, 2], P(('rep', 'shard')), may hold values from 1 to 192, 256 in all within a row
- norm_gain: float32 [1024], P('shard'), may hold values from 0.5 to 1.5
- in_weight: bfloat16 [1024, 4384], P('shard'), may hold values from -0.1875 to 0.1875
- conv_weight: float32 [2304, 4], P('shard'), may hold values from -3 to 3
- conv_bias: float32 [2304], P('shard'), may hold values from -0.5 to 0.5
- step_bias: float32 [32], P('shard'), may hold values from -6.9 to -2.3
- decay_log: float32 [32], P('shard'), may hold values from 0 to 2.77
- skip_gain: float32 [32], P('shard'), may hold values from 0.5 to 1.5
- gate_gain: float32 [2048], P('shard'), may hold values from 0.5 to 1.5
- out_weight: bfloat16 [2048, 1024], P('shard'), may hold values from -0.125 to 0.125
Outputs:
- layer_out: float32 [32768, 1024], P(('rep', 'shard'))
- input_grad: float32 [32768, 1024], P(('rep', 'shard'))
- norm_gain_grad: float32 [1024], P('shard')
- in_weight_grad: float32 [1024, 4384], P('shard')
- conv_weight_grad: float32 [2304, 4], P('shard')
- conv_bias_grad: float32 [2304], P('shard')
- step_bias_grad: float32 [32], P('shard')
- decay_log_grad: float32 [32], P('shard')
- skip_gain_grad: float32 [32], P('shard')
- gate_gain_grad: float32 [2048], P('shard')
- out_weight_grad: float32 [2048, 1024], P('shard')
Inputs may be any that keep to these rules, and one draw needn't show every extreme that they name: `seq_lengths`: each device's row of 2 lengths sums to 256.
All inputs are finite; a program needn't handle non-finite values.
Results may differ from a plain program's by a relative error of at most 0.0064.
Values may be sent and summed in bfloat16 or wider, within the bound.
No kernel may reach another device: no remote copies, remote signals or barrier semaphores. Data moves between devices by JAX's collectives and lax.ppermute only.
A program may use at most 128 MiB of HBM per device.

v0:
```python
import math
import jax
import jax.numpy as jnp
from jax import lax
from jax.sharding import Mesh
from jax.sharding import PartitionSpec as P

SPAN = 256
SHARD = ("shard_0", "shard_1")
REP = ("rep_hi", "core")
REP_SHARD = ("rep_hi", "core", "shard_0", "shard_1")
ALL = REP_SHARD
EPS = 1e-05
HIGH = lax.Precision.HIGHEST


def side_by_side(arrays, axis, dim, along):
    widths = [math.prod(a.shape[along:]) for a in arrays]
    both = jnp.concatenate(
        [a.reshape(*a.shape[:along], w) for a, w in zip(arrays, widths)], axis=along
    )
    result = lax.all_gather(both, axis, axis=dim, tiled=True)
    blocks = jnp.split(result, [sum(widths[:k]) for k in range(1, len(widths))], axis=along)
    return tuple(
        (b.reshape(*result.shape[:along], *a.shape[along:]) for a, b in zip(arrays, blocks))
    )


def sum_by_axis(total, axes):
    for axis in axes:
        total = lax.psum_scatter(total, axis, scatter_dimension=0, tiled=True)
    return total


def in_blocks(shard, dim, size):
    before, after = (shard.shape[:dim], shard.shape[dim + 1 :])
    return jnp.moveaxis(shard.reshape(*before, size, -1, *after), dim, 0)


def sum_at_owner(shard, axis, dim):
    size = lax.axis_size(axis)
    blocks = lax.all_to_all(in_blocks(shard, dim, size), axis, 0, 0, tiled=True)
    return jnp.sum(blocks, axis=0)


def sent_together(arrays, axis, dim, along):
    widths = [math.prod(a.shape[along:]) for a in arrays]
    both = jnp.concatenate(
        [a.reshape(*a.shape[:along], w) for a, w in zip(arrays, widths)], axis=along
    )
    result = sum_at_owner(both, axis, dim)
    blocks = jnp.split(result, [sum(widths[:k]) for k in range(1, len(widths))], axis=along)
    return tuple(
        (b.reshape(*result.shape[:along], *a.shape[along:]) for a, b in zip(arrays, blocks))
    )


def shifted(values, lag):
    zeros_top = jnp.zeros((lag,) + values.shape[1:], values.dtype)
    return jnp.concatenate([zeros_top, values[:-lag]], axis=0)


def segment_ids(lengths_row, count):
    offsets = jnp.cumsum(lengths_row, dtype=jnp.int32) - lengths_row
    places = jnp.arange(count, dtype=jnp.int32)
    return (
        jnp.sum((places[:, None] >= offsets[None, :]).astype(jnp.int32), axis=1, dtype=jnp.int32)
        - 1
    )


def row_product(left, right):
    return lax.dot_general(
        left, right, (((0,), (0,)), ((), ())), preferred_element_type=jnp.float32
    )


def back_product(left, right):
    return lax.dot_general(
        left, right, (((1,), (1,)), ((), ())), preferred_element_type=jnp.float32
    )


def norm_input(inputs, gain_one):
    scaling = lax.rsqrt(jnp.mean(inputs * inputs, axis=1, keepdims=True) + EPS)
    return inputs * scaling * gain_one[None, :]


def mixer(projected, segment, conv_weight, conv_bias, step_bias, decay_log, skip_gain, gate_gain):
    count = projected.shape[0]
    inner = gate_gain.shape[0]
    heads = step_bias.shape[0]
    head_dim = inner // heads
    channels = conv_weight.shape[0]
    state_dim = (channels - inner) // 2
    taps = conv_weight.shape[1]
    gate_part = projected[:, :inner]
    conv_in = projected[:, inner : inner + channels]
    step_raw = projected[:, inner + channels :]
    places = jnp.arange(count, dtype=jnp.int32)
    conv_out = conv_bias[None, :] + conv_weight[:, taps - 1][None, :] * conv_in
    for lag in range(1, taps):
        same = (shifted(segment, lag) == segment) & (places >= lag)
        conv_out = conv_out + jnp.where(
            same[:, None], conv_weight[:, taps - 1 - lag][None, :] * shifted(conv_in, lag), 0.0
        )
    activated = jax.nn.silu(conv_out)
    values = activated[:, :inner].reshape(count, heads, head_dim)
    b_matrix = activated[:, inner : inner + state_dim]
    c_matrix = activated[:, inner + state_dim :]
    step_size = jax.nn.softplus(step_raw + step_bias[None, :])
    decay = -jnp.exp(decay_log)[None, :] * step_size
    blocks = count // SPAN
    values_c = values.reshape(blocks, SPAN, heads, head_dim)
    b_spans = b_matrix.reshape(blocks, SPAN, state_dim)
    c_spans = c_matrix.reshape(blocks, SPAN, state_dim)
    step_c = step_size.reshape(blocks, SPAN, heads)
    cumul = jnp.cumsum(decay.reshape(blocks, SPAN, heads), axis=1)
    seg_c = segment.reshape(blocks, SPAN)
    rows_in = jnp.arange(SPAN, dtype=jnp.int32)
    lower = rows_in[:, None] >= rows_in[None, :]
    allowed = lower[None] & (seg_c[:, :, None] == seg_c[:, None, :])
    cumul_t = jnp.transpose(cumul, (0, 2, 1))
    differ = cumul_t[:, :, :, None] - cumul_t[:, :, None, :]
    weights_l = jnp.exp(jnp.where(allowed[:, None], differ, -10000.0))
    scores = jnp.einsum("cin,cjn->cij", c_spans, b_spans, precision=HIGH)
    mixing = weights_l * scores[:, None]
    scaled_in = values_c * step_c[..., None]
    y_intra = jnp.einsum("chij,cjhp->cihp", mixing, scaled_in, precision=HIGH)
    carried = jnp.zeros((heads, head_dim, state_dim), jnp.float32)
    before_seg = jnp.int32(-1)
    linked = (seg_c[0] == before_seg).astype(jnp.float32)
    reach = jnp.exp(cumul[0]) * linked[:, None]
    inter = jnp.einsum("in,hpn->ihp", c_spans[0], carried, precision=HIGH) * reach[:, :, None]
    pieces = [y_intra[0] + inter]
    y_all = jnp.concatenate(pieces, axis=0) + skip_gain[None, :, None] * values
    gated_pre = y_all.reshape(count, inner) * jax.nn.silu(gate_part)
    scaling = lax.rsqrt(jnp.mean(gated_pre * gated_pre, axis=1, keepdims=True) + EPS)
    return gated_pre * scaling * gate_gain[None, :]


def gather_rows(weight):
    rows = weight.shape[0]
    half = rows // 2
    core = lax.axis_index("core")
    mine = lax.dynamic_slice_in_dim(weight, core * half, half, axis=0)
    part = lax.all_gather(mine, SHARD, axis=0, tiled=False)
    both = lax.all_gather(part, "core", axis=1, tiled=False)
    return both.reshape(-1, weight.shape[1])


def reduce_rows(partial):
    groups = lax.axis_size(SHARD)
    cols = partial.shape[1]
    blocks = partial.reshape(groups, 2, -1, cols)
    halves = lax.psum_scatter(blocks, "core", scatter_dimension=1, tiled=False)
    owned = lax.psum_scatter(halves, SHARD, scatter_dimension=0, tiled=False)
    owned = lax.psum(owned, "rep_hi")
    return lax.all_gather(owned, "core", axis=0, tiled=True)


def on_device(
    layer_in,
    cotangent,
    seq_lengths,
    norm_gain,
    in_weight,
    conv_weight,
    conv_bias,
    step_bias,
    decay_log,
    skip_gain,
    gate_gain,
    out_weight,
):
    count = layer_in.shape[0]
    groups = lax.axis_size(SHARD)
    segment = segment_ids(seq_lengths[0], count)
    smalls = (norm_gain, conv_weight, conv_bias, step_bias, decay_log, skip_gain, gate_gain)
    flat = jnp.concatenate([a.reshape(-1) for a in smalls])
    flat_all = lax.all_gather(flat, SHARD, axis=0, tiled=False)
    pieces_full = []
    offset = 0
    for a in smalls:
        size = a.size
        block = flat_all[:, offset : offset + size]
        pieces_full.append(block.reshape((groups * a.shape[0],) + a.shape[1:]))
        offset += size
    norm_full, convw_full, convb_full, stepb_full, decay_full, skip_full, gategain_full = (
        pieces_full
    )
    normed_f, norm_back = jax.vjp(norm_input, layer_in, norm_full)
    normed = normed_f.astype(jnp.bfloat16)
    in_whole = gather_rows(in_weight)
    out_whole = gather_rows(out_weight)
    projected = jnp.dot(normed, in_whole, preferred_element_type=jnp.float32)

    def bound_mixer(proj_arg, cw_arg, cb_arg, sb_arg, dl_arg, sk_arg, gg_arg):
        return mixer(proj_arg, segment, cw_arg, cb_arg, sb_arg, dl_arg, sk_arg, gg_arg)

    gated_f, mixer_back = jax.vjp(
        bound_mixer,
        projected,
        convw_full,
        convb_full,
        stepb_full,
        decay_full,
        skip_full,
        gategain_full,
    )
    gated = gated_f.astype(jnp.bfloat16)
    branch_out = jnp.dot(gated, out_whole, preferred_element_type=jnp.float32)
    layer_out = layer_in + branch_out
    cot_low = cotangent.astype(jnp.bfloat16)
    out_owned = reduce_rows(row_product(gated, cot_low))
    gated_grad = back_product(cot_low, out_whole)
    proj_grad, g_convw, g_convb, g_stepb, g_decay, g_skip, g_gategain = mixer_back(gated_grad)
    proj_low = proj_grad.astype(jnp.bfloat16)
    cols = proj_low.shape[1]
    wide = -(-cols // 128) * 128
    proj_wide = jnp.pad(proj_low, ((0, 0), (0, wide - cols)))
    in_owned = reduce_rows(row_product(normed, proj_wide))[:, :cols]
    normed_grad = back_product(proj_low, in_whole)
    back_in, g_norm = norm_back(normed_grad)
    input_grad = cotangent + back_in
    grads = (g_norm, g_convw, g_convb, g_stepb, g_decay, g_skip, g_gategain)
    small_blocks = jnp.concatenate([g.reshape(groups, -1) for g in grads], axis=1)
    small_sum = lax.psum(small_blocks, ALL)
    mine = lax.dynamic_index_in_dim(small_sum, lax.axis_index(SHARD), axis=0, keepdims=False)
    small_final = []
    offset = 0
    for g in grads:
        size = g.size // groups
        small_final.append(
            mine[offset : offset + size].reshape((g.shape[0] // groups,) + g.shape[1:])
        )
        offset += size
    return (
        layer_out,
        input_grad,
        small_final[0],
        in_owned,
        small_final[1],
        small_final[2],
        small_final[3],
        small_final[4],
        small_final[5],
        small_final[6],
        out_owned,
    )


def solution(mesh):
    split = Mesh(
        mesh.devices.reshape(mesh.shape["rep"] // 2, 2, 4, 2),
        ("rep_hi", "core", "shard_0", "shard_1"),
    )
    in_specs = (
        P(REP_SHARD, None),
        P(REP_SHARD, None),
        P(REP_SHARD, None),
        P(SHARD),
        P(SHARD, None),
        P(SHARD, None),
        P(SHARD),
        P(SHARD),
        P(SHARD),
        P(SHARD),
        P(SHARD),
        P(SHARD, None),
    )
    out_specs = (
        P(REP_SHARD, None),
        P(REP_SHARD, None),
        P(SHARD),
        P(SHARD, None),
        P(SHARD, None),
        P(SHARD),
        P(SHARD),
        P(SHARD),
        P(SHARD),
        P(SHARD),
        P(SHARD, None),
    )
    return jax.shard_map(
        on_device, mesh=split, in_specs=in_specs, out_specs=out_specs, check_vma=False
    )
```

profile of v0, /device:TPU:1, one launch (start us, length us, event | category | flops | bytes accessed | tf_op | source)
XLA Modules:
  0.0 826.9 jit_solution(1690237678751658720)
XLA Ops:
  7.3 1.2 copy-done
  8.8 1.6 copy.77
  10.5 0.7 constant_dynamic-slice_fusion.1
  11.3 100.5 %all-gather.16.cloned.1.call-done = bf16[512,4384]{1,0:T(8,128)(2,1)} async-done(((bf16[64,4384]{1,0:T(8,128)(2,1)}), bf16[512,4384]{1,0:T(8,128)(2,1)}) %all-gather.16.cloned.1.call-update) | async-done | bytes 4489232 | tf_op jit(solution)/shard_map/all_gather | solution.py:147
  114.2 26.8 %all-reduce.19 = f32[14688]{0:T(1024)S(1)} all-reduce(f32[14688]{0:T(1024)S(1)} %dynamic-update-slice), channel_id=2, replica_groups=mesh['rep_hi'=8,'core'=2,'shard_0'=4,'shard_1'=2] {'shard_0','shard_1'}, use_global_device_ids=true, to_apply=%add.19 | all-reduce | flops 14688 | bytes 117504
  141.7 1.2 reshape.539
  143.2 2.2 slice_reduce_fusion.3
  145.6 0.7 fusion.50
  146.4 21.5 %all-gather.20.cloned.1.call-done = bf16[1024,1024]{1,0:T(8,128)(2,1)} async-done(((bf16[128,1024]{1,0:T(8,128)(2,1)}), bf16[1024,1024]{1,0:T(8,128)(2,1)}) %all-gather.20.cloned.1.call-update) | async-done | bytes 2097168 | tf_op jit(solution)/shard_map/all_gather | solution.py:147
  168.0 25.5 %all-gather.18.cloned.1.call-done = bf16[8,128,4384]{2,1,0:T(8,128)(2,1)} async-done(((bf16[8,64,4384]{2,1,0:T(8,128)(2,1)}), bf16[8,128,4384]{2,1,0:T(8,128)(2,1)}) %all-gather.18.cloned.1.call-update) | async-done | bytes 8978448 | tf_op jit(solution)/shard_map/all_gather | solution.py:148
  193.4 7.5 fusion.74
  201.0 2.1 copy-done.2
  203.1 0.7 multiply_bitcast_fusion
  204.6 3.7 slice.178
  208.3 1.0 copy-done.3
  209.3 1.5 slice.176
  210.9 1.6 slice.174
  212.6 7.5 fusion.19
  221.6 1.8 fusion.45
  223.4 1.4 copy-done.17
  224.8 9.2 %fusion.24 = f32[256,32,64]{0,2,1:T(8,128)S(1)} fusion(f32[256,32,64]{0,2,1:T(8,128)S(1)} %bitcast.148, f32[256,32,64]{0,2,1:T(8,128)S(1)} %fusion.45, f32[256,256]{1,0:T(8,128)S(1)} %fusion.53, f32[32,256]{1,0:T(8,128)S(1)} %bitcast_add_fusion.2, pred[256,256]{1,0:T(8,128)(4,1)S(1)} %copy-done.39, f32[32]{0:T(128)S(1)} %mul.424, ...), kind=kOutput, calls=%fused_computation.41 | convolution fusion | flops 1619525632 | bytes 6717568 | tf_op jit(solution)/shard_map/jvp(chij,cjhp->cihp)/dot_general | solution.py:129
  234.0 3.1 multiply_reduce_fusion.9
  237.1 1.3 fusion.47
  238.4 14.0 %copy.71 = f32[8,2,128,1024]{3,2,0,1:T(8,128)} copy(f32[8,2,128,1024]{3,2,1,0:T(8,128)S(1)} %bitcast.137) | data formatting | bytes 16777216 | tf_op jit(solution)/shard_map/reshape | solution.py:155
  252.5 0.7 mul.455
  253.2 4.8 multiply_reduce_fusion.5
  258.1 4.1 multiply_reduce_fusion.6
  262.2 11.4 %fusion.6 = (f32[32,256]{1,0:T(8,128)S(1)}, f32[32,256]{1,0:T(8,128)S(1)}, f32[256,256]{1,0:T(8,128)S(1)}) fusion(f32[256,256]{1,0:T(8,128)S(1)} %copy-done.25, f32[32,256]{1,0:T(8,128)S(1)} %copy-done.43, pred[256,256]{1,0:T(8,128)(4,1)S(1)} %copy-done.40, f32[32,64,256]{2,1,0:T(8,128)S(1)} %bitcast.138, f32[256,32,64]{0,2,1:T(8,128)S(1)} %bitcast.150, ...), kind=kOutput, calls=%fused_computation.7 | convolution fusion | flops 1629929472 | bytes 4915200 | tf_op jit(solution)/shard_map/transpose(jvp(chij,cjhp->cihp))/dot_general | solution.py:129
  275.0 3.2 reduce-window.19
  278.2 0.7 slice_reduce_fusion.4
  278.8 1.3 reduce-window.24
  280.1 1.2 slice_bitcast_fusion.2
  281.4 1.4 copy.68
  282.7 1.4 broadcast.255
  284.1 1.4 reshape.560
  285.5 3.0 fusion.36
  288.7 9.0 %fusion.25 = (f32[256,32]{0,1:T(8,128)S(1)}, f32[1,256,32,64]{1,3,2,0:T(8,128)S(1)}) fusion(f32[1,256,32,64]{1,3,2,0:T(8,128)} %bitcast.149, f32[256,32]{0,1:T(8,128)} %get-tuple-element.73, f32[32,64,256]{2,1,0:T(8,128)} %bitcast.140, f32[256,256]{1,0:T(8,128)} %copy-done.24, f32[32,256]{1,0:T(8,128)} %copy-done.42, pred[256,256]{1,0:T(8,128)(4,1)} %fusion.50), kind=kOutput, calls=%fused_computation.45 | convolution fusion | flops 1618468864 | bytes 6717440 | tf_op jit(solution)/shard_map/transpose(jvp(chij,cjhp->cihp))/dot_general | solution.py:129
  297.9 1.2 fusion.55
  299.2 1.3 convolution_add_fusion.1
  300.9 1.3 copy-done.10
  302.2 0.7 copy-done.12
  302.9 2.4 multiply_reduce_fusion.4
  305.3 2.3 multiply_reduce_fusion.3
  307.6 1.0 slice_multiply_fusion.1
  308.6 1.0 slice_multiply_fusion
  309.6 1.0 slice_multiply_fusion.2
  310.6 1.8 fusion.75
  313.2 2.8 fusion.20
  316.0 6.6 copy.70
  322.7 0.7 reduce-scatter.11.cloned.1.call-update
  323.4 31.1 %reduce-scatter.5.cloned.1.call-done = f32[8,1,64,4480]{3,2,0,1:T(8,128)} async-done(((f32[8,2,64,4480]{3,2,0,1:T(8,128)}), f32[8,1,64,4480]{3,2,0,1:T(8,128)}) %reduce-scatter.5.cloned.1.call-update) | async-done | bytes 9175056 | tf_op jit(solution)/shard_map/reduce_scatter | solution.py:156
  354.6 94.9 %reduce-scatter.11.cloned.1.call-done = f32[1,128,1024]{2,1,0:T(8,128)} async-done(((f32[8,128,1024]{2,1,0:T(8,128)}), f32[1,128,1024]{2,1,0:T(8,128)}) %reduce-scatter.11.cloned.1.call-update) | async-done | bytes 524304 | tf_op jit(solution)/shard_map/reduce_scatter | solution.py:157
  449.4 186.6 %reduce-scatter.7.cloned.1.call-done = f32[1,64,4480]{2,1,0:T(8,128)} async-done(((f32[8,64,4480]{2,1,0:T(8,128)}), f32[1,64,4480]{2,1,0:T(8,128)}) %reduce-scatter.7.cloned.1.call-update) | async-done | bytes 1146896 | tf_op jit(solution)/shard_map/reduce_scatter | solution.py:157
  636.1 89.9 %all-reduce.23.cloned.1.call-done = (f32[64,4480]{1,0:T(8,128)}, f32[128,1024]{1,0:T(8,128)}) async-done(((f32[64,4480]{1,0:T(8,128)}, f32[128,1024]{1,0:T(8,128)}), (f32[64,4480]{1,0:T(8,128)}, f32[128,1024]{1,0:T(8,128)})) %all-reduce.23.cloned.1.call-update) | async-done | bytes 1671184 | tf_op jit(solution)/shard_map/psum | solution.py:158
  727.3 1.4 copy.69
  728.7 2.0 reshape.564
  730.8 7.9 multiply_reduce_fusion.10
  738.8 68.5 %psum.21 = f32[8,1836]{1,0:T(8,128)S(1)} all-reduce(f32[8,1836]{1,0:T(8,128)S(1)} %concatenate.35), channel_id=1, replica_groups=mesh['rep_hi'=8,'core'=2,'shard_0'=4,'shard_1'=2] {'rep_hi','core','shar..., use_global_device_ids=true, to_apply=%region_26.27 | all-reduce | flops 14688 | bytes 117504 | tf_op jit(solution)/shard_map/psum | solution.py:228
  808.1 0.7 copy.73
  808.8 0.7 dynamic-slice_reduce_fusion.1
  810.6 2.8 fusion.39
  813.4 2.4 convolution_add_fusion
  815.8 3.2 copy.72
  819.0 1.0 copy.98
  (238 shorter events, 12.0 us)
Async XLA Ops:
  7.2 3.3 copy-start.29
  7.2 104.6 %all-gather.16.cloned.1.call-start = ((), (), s32[]{:S(2)}) async-start(), calls=%async_computation.10 | async-start | bytes 5160960 | tf_op jit(solution)/shard_map/all_gather | solution.py:147
  10.5 157.4 %all-gather.20.cloned.1.call-start = ((), (), s32[]{:S(2)}) async-start(), calls=%async_computation.12 | async-start | bytes 2359296 | tf_op jit(solution)/shard_map/all_gather | solution.py:147
  11.3 100.7 %copy-start.53 = (f32[288,4]{0,1:T(4,128)S(1)}, f32[288,4]{0,1:T(4,128)}, u32[]{:S(2)}) copy-start(f32[288,4]{0,1:T(4,128)} %param.17) | copy-start | bytes 13828
  11.3 182.1 %all-gather.18.cloned.1.call-start = ((), (), s32[]{:S(2)}) async-start(), calls=%async_computation.11 | async-start | bytes 13762560 | tf_op jit(solution)/shard_map/all_gather | solution.py:148
  111.8 29.2 %copy-start.70 = (s32[1,2]{1,0:T(1,128)S(1)}, s32[1,2]{1,0:T(1,128)}, u32[]{:S(2)}) copy-start(s32[1,2]{1,0:T(1,128)} %param.14) | copy-start | bytes 28
  111.9 31.2 %copy-start.11 = (f32[256,1024]{1,0:T(8,128)S(1)}, f32[256,1024]{1,0:T(8,128)}, u32[]{:S(2)}) copy-start(f32[256,1024]{1,0:T(8,128)} %param.12) | copy-start | bytes 3145732
  111.9 141.3 %all-gather.22.cloned.1.call-start = ((), (), s32[]{:S(2)}) async-start(), calls=%async_computation.13 | async-start | bytes 6291456 | tf_op jit(solution)/shard_map/all_gather | solution.py:148
  141.6 59.3 %copy-start.60 = (f32[32]{0:T(128)}, f32[32]{0:T(128)S(1)}, u32[]{:S(2)}) copy-start(f32[32]{0:T(128)S(1)} %neg.39) | copy-start | bytes 388
  141.7 59.2 %copy-start.62 = (f32[32]{0:T(128)}, f32[32]{0:T(128)S(1)}, u32[]{:S(2)}) copy-start(f32[32]{0:T(128)S(1)} %add.163) | copy-start | bytes 388
  145.4 67.1 %copy-start.31 = (f32[2304]{0:T(1024)}, f32[2304]{0:T(1024)S(1)}, u32[]{:S(2)}) copy-start(f32[2304]{0:T(1024)S(1)} %get-tuple-element.53) | copy-start | bytes 27652
  145.4 67.1 %copy-start.33 = (f32[2304]{0:T(1024)}, f32[2304]{0:T(1024)S(1)}, u32[]{:S(2)}) copy-start(f32[2304]{0:T(1024)S(1)} %get-tuple-element.54) | copy-start | bytes 27652
  145.4 67.1 %copy-start.35 = (f32[2304]{0:T(1024)}, f32[2304]{0:T(1024)S(1)}, u32[]{:S(2)}) copy-start(f32[2304]{0:T(1024)S(1)} %get-tuple-element.56) | copy-start | bytes 27652
  145.5 67.1 %copy-start.37 = (f32[2304]{0:T(1024)}, f32[2304]{0:T(1024)S(1)}, u32[]{:S(2)}) copy-start(f32[2304]{0:T(1024)S(1)} %get-tuple-element.55) | copy-start | bytes 27652
  145.5 47.9 %copy-start.44 = (f32[256]{0:T(256)}, f32[256]{0:T(256)S(1)}, u32[]{:S(2)}) copy-start(f32[256]{0:T(256)S(1)} %fusion.66) | copy-start | bytes 3076
  145.6 67.0 %copy-start.54 = (pred[256]{0:T(512)(128)(4,1)}, pred[256]{0:T(512)(128)(4,1)S(1)}, u32[]{:S(2)}) copy-start(pred[256]{0:T(512)(128)(4,1)S(1)} %get-tuple-element.90) | copy-start | bytes 772
  145.6 67.0 %copy-start.56 = (pred[256]{0:T(512)(128)(4,1)}, pred[256]{0:T(512)(128)(4,1)S(1)}, u32[]{:S(2)}) copy-start(pred[256]{0:T(512)(128)(4,1)S(1)} %get-tuple-element.91) | copy-start | bytes 772
  145.6 67.0 %copy-start.58 = (pred[256]{0:T(512)(128)(4,1)}, pred[256]{0:T(512)(128)(4,1)S(1)}, u32[]{:S(2)}) copy-start(pred[256]{0:T(512)(128)(4,1)S(1)} %get-tuple-element.92) | copy-start | bytes 772
  145.6 74.8 %copy-start.48 = (f32[256]{0:T(256)}, f32[256]{0:T(256)S(1)}, u32[]{:S(2)}) copy-start(f32[256]{0:T(256)S(1)} %get-tuple-element.89) | copy-start | bytes 3076
  167.9 154.8 %reduce-scatter.9.cloned.1.call-start = ((), (), s32[]{:S(2)}) async-start(), calls=%async_computation.7 | async-start | bytes 12582912 | tf_op jit(solution)/shard_map/reduce_scatter | solution.py:156
  204.6 4.7 copy-start.3
  220.2 13.7 %copy-start.21 = (f32[256,2048]{0,1:T(8,128)}, f32[256,2048]{0,1:T(8,128)S(1)}, u32[]{:S(2)}) copy-start(f32[256,2048]{0,1:T(8,128)S(1)} %slice.179) | copy-start | bytes 6291460
  220.3 4.5 copy-start.26
  220.3 4.5 copy-start.39
  220.5 13.5 %copy-start.42 = (f32[32,256]{1,0:T(8,128)}, f32[32,256]{1,0:T(8,128)S(1)}, u32[]{:S(2)}) copy-start(f32[32,256]{1,0:T(8,128)S(1)} %bitcast_add_fusion.2) | copy-start | bytes 98308
  221.5 12.4 %copy-start.24 = (f32[256,256]{1,0:T(8,128)}, f32[256,256]{1,0:T(8,128)S(1)}, u32[]{:S(2)}) copy-start(f32[256,256]{1,0:T(8,128)S(1)} %fusion.53) | copy-start | bytes 786436
  234.0 3.1 copy-start.15
  234.0 3.1 copy-start.19
  237.1 20.9 %copy-start.46 = (f32[256]{0:T(256)}, f32[256]{0:T(256)S(1)}, u32[]{:S(2)}) copy-start(f32[256]{0:T(256)S(1)} %fusion.67) | copy-start | bytes 3076
  252.4 102.1 %reduce-scatter.5.cloned.1.call-start = ((), (), s32[]{:S(2)}) async-start(), calls=%async_computation.4 | async-start | bytes 27525120 | tf_op jit(solution)/shard_map/reduce_scatter | solution.py:156
  253.2 4.8 copy-start.7
  253.2 4.8 copy-start.16
  258.0 4.2 copy-start.22
  258.1 4.2 copy-start.25
  258.1 4.1 copy-start.27
  258.1 4.1 copy-start.40
  258.1 4.1 copy-start.43
  262.2 11.4 %copy-start.4 = (f32[256,2048]{0,1:T(8,128)}, f32[256,2048]{0,1:T(8,128)S(1)}, u32[]{:S(2)}) copy-start(f32[256,2048]{0,1:T(8,128)S(1)} %get-tuple-element.60) | copy-start | bytes 6291460
  262.2 11.4 %copy-start.18 = (f32[256,32,64]{0,2,1:T(8,128)S(1)}, f32[256,32,64]{0,2,1:T(8,128)}, u32[]{:S(2)}) copy-start(f32[256,32,64]{0,2,1:T(8,128)} %copy-done.17) | copy-start | bytes 6291460
  285.5 12.1 %slice-start = ((s8[4489216]{0:T(1024)(128)(4,1)}), s8[4194304]{0:T(1024)(128)(4,1)S(1)}, s32[]{:S(2)}) async-start(s8[4489216]{0:T(1024)(128)(4,1)} %bitcast.135), calls=%async_computation.15 | async-start | bytes 8388608
  288.6 9.1 %slice-start.1 = ((s8[4489216]{0:T(1024)(128)(4,1)}), s8[294912]{0:T(1024)(128)(4,1)S(1)}, s32[]{:S(2)}) async-start(s8[4489216]{0:T(1024)(128)(4,1)} %bitcast.135), calls=%async_computation.16 | async-start | bytes 589824
  288.6 9.1 %copy-start.28 = (f32[256,32]{0,1:T(8,128)S(1)}, f32[256,32]{0,1:T(8,128)}, u32[]{:S(2)}) copy-start(f32[256,32]{0,1:T(8,128)} %get-tuple-element.73) | copy-start | bytes 98308
  288.6 9.1 %copy-start.30 = (f32[1,32,256]{2,1,0:T(8,128)S(1)}, f32[1,32,256]{2,1,0:T(8,128)}, u32[]{:S(2)}) copy-start(f32[1,32,256]{2,1,0:T(8,128)} %reshape.560) | copy-start | bytes 98308
  288.6 9.1 %copy-start.61 = (f32[32]{0:T(128)S(1)}, f32[32]{0:T(128)}, u32[]{:S(2)}) copy-start(f32[32]{0:T(128)} %copy-done.60) | copy-start | bytes 388
  288.6 9.1 %copy-start.63 = (f32[32]{0:T(128)S(1)}, f32[32]{0:T(128)}, u32[]{:S(2)}) copy-start(f32[32]{0:T(128)} %copy-done.62) | copy-start | bytes 388
  288.6 11.8 %copy-start.5 = (f32[256,2048]{0,1:T(8,128)S(1)}, f32[256,2048]{0,1:T(8,128)}, u32[]{:S(2)}) copy-start(f32[256,2048]{0,1:T(8,128)} %copy-done.4) | copy-start | bytes 6291460
  288.6 11.8 %copy-start.41 = (f32[2048]{0:T(1024)S(1)}, f32[2048]{0:T(1024)}, u32[]{:S(2)}) copy-start(f32[2048]{0:T(1024)} %mul.455) | copy-start | bytes 24580
  300.5 2.4 copy-start.12
  302.9 2.4 copy-start.8
  302.9 2.4 copy-start.9
  302.9 2.4 copy-start.55
  302.9 2.4 copy-start.57
  313.2 2.8 copy-start.13
  322.6 126.8 %reduce-scatter.11.cloned.1.call-start = ((), (), s32[]{:S(2)}) async-start(), calls=%async_computation.8 | async-start | bytes 4718592 | tf_op jit(solution)/shard_map/reduce_scatter | solution.py:157
  323.4 312.6 %reduce-scatter.7.cloned.1.call-start = ((), (), s32[]{:S(2)}) async-start(), calls=%async_computation.5 | async-start | bytes 10321920 | tf_op jit(solution)/shard_map/reduce_scatter | solution.py:157
  354.5 372.4 %copy-start.52 = (f32[2048]{0:T(1024)S(1)}, f32[2048]{0:T(1024)}, u32[]{:S(2)}) copy-start(f32[2048]{0:T(1024)} %get-tuple-element.47) | copy-start | bytes 24580
  354.5 371.5 %all-reduce.23.cloned.1.call-start = ((), (), s32[]{:S(2)}) async-start(), calls=%async_computation.14 | async-start | bytes 3342336 | tf_op jit(solution)/shard_map/psum | solution.py:158
  636.0 179.8 %all-gather.14.cloned.1.call-start = ((), (), s32[]{:S(2)}) async-start(), calls=%async_computation.9 | async-start | bytes 1572864 | tf_op jit(solution)/shard_map/all_gather | solution.py:159
  726.0 89.8 %all-gather.12.cloned.1.call-start = ((), (), s32[]{:S(2)}) async-start(), calls=%async_computation.6 | async-start | bytes 3440640 | tf_op jit(solution)/shard_map/all_gather | solution.py:159
  730.8 79.9 %copy-start.51 = (f32[256]{0:T(256)S(1)}, f32[256]{0:T(256)}, u32[]{:S(2)}) copy-start(f32[256]{0:T(256)} %copy-done.50) | copy-start | bytes 3076
  738.8 74.6 %copy-start.47 = (f32[256]{0:T(256)S(1)}, f32[256]{0:T(256)}, u32[]{:S(2)}) copy-start(f32[256]{0:T(256)} %copy-done.46) | copy-start | bytes 3076
  808.8 4.6 copy-start.20
  815.8 3.2 copy-start.23
  815.8 4.1 copy-start.1
  (21 other events, 33.2 us)
Sparse Core Ops, SparseCore 0:
  10.6 101.1 all-gather.15
  114.0 53.8 all-gather.19
  169.6 23.8 all-gather.17
  194.9 17.6 all-gather.21
  252.5 20.8 reduce-scatter.8
  322.8 31.6 reduce-scatter.4
  357.0 92.3 reduce-scatter.10
  452.0 183.9 reduce-scatter.6
  638.8 87.1 all-reduce.22
  727.5 15.0 all-gather.13
  744.3 14.8 all-gather.11
where the time goes:
time: 835 us; the launch traced here: 827 us
  waiting for transfers between devices  551 us (66%)
  blocking collectives  95.2 us (11%)
  local copies, waits for them, and re-layouts  64.2 us (8%)
  matrix products  64 us (8%)
  other arithmetic  35.6 us (4%)
  between operations  16.2 us (2%)
    reduce_scatter x2, waiting for transfers between devices, reduce_rows(): owned = lax.psum_scatter(halves, SHARD, scatter_dimension=0, tiled=False)  281 us
    all_gather x2, waiting for transfers between devices, gather_rows(): part = lax.all_gather(mine, SHARD, axis=0, tiled=False)  122 us
    psum x1, waiting for transfers between devices, reduce_rows(): owned = lax.psum(owned, 'rep_hi')  89.9 us
    psum x1, blocking collectives, on_device(): small_sum = lax.psum(small_blocks, ALL)  68.5 us
    reduce_scatter x2, waiting for transfers between devices, reduce_rows(): halves = lax.psum_scatter(blocks, 'core', scatter_dimension=1, tiled=False)  31.1 us
    dot_general x3, matrix products, mixer(): y_intra = jnp.einsum('chij,cjhp->cihp', mixing, scaled_in, precision=HIGH)  29.5 us
    unnamed x1, blocking collectives  26.8 us
    all_gather x2, waiting for transfers between devices, gather_rows(): both = lax.all_gather(part, 'core', axis=1, tiled=False)  25.5 us
  transfers between devices with their start and end apart: 11, of which 7 were waited for; matrix products, arithmetic and copies ran while one was open for 18% of the time, Pallas kernels for 0%

commit v1 on v0

--- a/solution.py
+++ b/solution.py
@@ -225,7 +225,7 @@
     input_grad = cotangent + back_in
     grads = (g_norm, g_convw, g_convb, g_stepb, g_decay, g_skip, g_gategain)
     small_blocks = jnp.concatenate([g.reshape(groups, -1) for g in grads], axis=1)
-    small_sum = lax.psum(small_blocks, ALL)
+    small_sum = jnp.sum(lax.all_gather(small_blocks, ALL), axis=0)
     mine = lax.dynamic_index_in_dim(small_sum, lax.axis_index(SHARD), axis=0, keepdims=False)
     small_final = []
     offset = 0

time: 835 us -> 1090 us (1.31)
  waiting for transfers between devices: 551 us -> 872 us
  blocking collectives: 95.2 us -> 26.8 us
    all_gather x0 -> x1, waiting for transfers between devices: none -> 311 us  [on_device(): small_sum = jnp.sum(lax.all_gather(small_blocks, ALL), axis=0)]
    psum x1 -> x0, blocking collectives: 68.5 us -> none  [on_device(): small_sum = lax.psum(small_blocks, ALL)]
    all_gather x2, waiting for transfers between devices: 0.01 us -> 22.7 us  [reduce_rows(): return lax.all_gather(owned, 'core', axis=0, tiled=True)]
    psum x1, waiting for transfers between devices: 89.9 us -> 76.7 us  [reduce_rows(): owned = lax.psum(owned, 'rep_hi')]
  transfers between devices with their start and end apart: 11 -> 12, of which waited for: 7 -> 10; matrix products, arithmetic and copies ran while one was open for 18% -> 14% of each run, Pallas kernels for 0% -> 0%
where the time goes in v1:
time: 1090 us; the launch traced here: 1080 us
  waiting for transfers between devices  872 us (80%)
  local copies, waits for them, and re-layouts  64.8 us (6%)
  matrix products  64 us (6%)
  other arithmetic  39.4 us (4%)
  blocking collectives  26.8 us (2%)
  between operations  16.6 us (2%)
    all_gather x1, waiting for transfers between devices, on_device(): small_sum = jnp.sum(lax.all_gather(small_blocks, ALL), axis=0)  311 us
    reduce_scatter x2, waiting for transfers between devices, reduce_rows(): owned = lax.psum_scatter(halves, SHARD, scatter_dimension=0, tiled=False)  281 us
    all_gather x2, waiting for transfers between devices, gather_rows(): part = lax.all_gather(mine, SHARD, axis=0, tiled=False)  122 us
    psum x1, waiting for transfers between devices, reduce_rows(): owned = lax.psum(owned, 'rep_hi')  76.7 us
    reduce_scatter x2, waiting for transfers between devices, reduce_rows(): halves = lax.psum_scatter(blocks, 'core', scatter_dimension=1, tiled=False)  31.1 us
    dot_general x3, matrix products, mixer(): y_intra = jnp.einsum('chij,cjhp->cihp', mixing, scaled_in, precision=HIGH)  29.5 us
    unnamed x1, blocking collectives  26.8 us
    all_gather x2, waiting for transfers between devices, gather_rows(): both = lax.all_gather(part, 'core', axis=1, tiled=False)  25.5 us
  transfers between devices with their start and end apart: 12, of which 10 were waited for; matrix products, arithmetic and copies ran while one was open for 14% of the time, Pallas kernels for 0%

profile of v1, /device:TPU:1, one launch (start us, length us, event | category | flops | bytes accessed | tf_op | source)
XLA Modules:
  0.0 1084.2 jit_solution(12530968779439841013)
XLA Ops:
  7.3 1.2 copy-done
  8.8 1.6 copy.77
  10.5 0.7 constant_dynamic-slice_fusion.1
  11.3 100.5 %all-gather.18.cloned.1.call-done = bf16[512,4384]{1,0:T(8,128)(2,1)} async-done(((bf16[64,4384]{1,0:T(8,128)(2,1)}), bf16[512,4384]{1,0:T(8,128)(2,1)}) %all-gather.18.cloned.1.call-update) | async-done | bytes 4489232 | tf_op jit(solution)/shard_map/all_gather | solution.py:147
  114.2 26.8 %all-reduce.19 = f32[14688]{0:T(1024)S(1)} all-reduce(f32[14688]{0:T(1024)S(1)} %dynamic-update-slice), channel_id=2, replica_groups=mesh['rep_hi'=8,'core'=2,'shard_0'=4,'shard_1'=2] {'shard_0','shard_1'}, use_global_device_ids=true, to_apply=%add.19 | all-reduce | flops 14688 | bytes 117504
  141.7 1.2 reshape.539
  143.2 2.2 slice_reduce_fusion.3
  145.6 0.7 fusion.50
  146.4 21.5 %all-gather.22.cloned.1.call-done = bf16[1024,1024]{1,0:T(8,128)(2,1)} async-done(((bf16[128,1024]{1,0:T(8,128)(2,1)}), bf16[1024,1024]{1,0:T(8,128)(2,1)}) %all-gather.22.cloned.1.call-update) | async-done | bytes 2097168 | tf_op jit(solution)/shard_map/all_gather | solution.py:147
  168.0 25.5 %all-gather.20.cloned.1.call-done = bf16[8,128,4384]{2,1,0:T(8,128)(2,1)} async-done(((bf16[8,64,4384]{2,1,0:T(8,128)(2,1)}), bf16[8,128,4384]{2,1,0:T(8,128)(2,1)}) %all-gather.20.cloned.1.call-update) | async-done | bytes 8978448 | tf_op jit(solution)/shard_map/all_gather | solution.py:148
  193.4 7.5 fusion.74
  201.0 2.1 copy-done.2
  203.1 0.7 multiply_bitcast_fusion
  204.6 3.7 slice.178
  208.3 1.0 copy-done.3
  209.3 1.5 slice.176
  210.9 1.6 slice.174
  212.6 7.5 fusion.19
  221.5 1.8 fusion.45
  223.3 1.4 copy-done.17
  224.8 9.2 fusion.24
  234.0 3.1 multiply_reduce_fusion.9
  237.1 1.3 fusion.47
  238.4 14.0 %copy.71 = f32[8,2,128,1024]{3,2,0,1:T(8,128)} copy(f32[8,2,128,1024]{3,2,1,0:T(8,128)S(1)} %bitcast.139) | data formatting | bytes 16777216 | tf_op jit(solution)/shard_map/reshape | solution.py:155
  253.2 4.8 multiply_reduce_fusion.5
  258.1 4.1 multiply_reduce_fusion.6
  262.2 11.4 %fusion.6 = (f32[32,256]{1,0:T(8,128)S(1)}, f32[32,256]{1,0:T(8,128)S(1)}, f32[256,256]{1,0:T(8,128)S(1)}) fusion(f32[256,256]{1,0:T(8,128)S(1)} %copy-done.25, f32[32,256]{1,0:T(8,128)S(1)} %copy-done.43, pred[256,256]{1,0:T(8,128)(4,1)S(1)} %copy-done.40, f32[32,64,256]{2,1,0:T(8,128)S(1)} %bitcast.140, f32[256,32,64]{0,2,1:T(8,128)S(1)} %bitcast.152, ...), kind=kOutput, calls=%fused_computation.8 | convolution fusion | flops 1629929472 | bytes 4915200 | tf_op jit(solution)/shard_map/transpose(jvp(chij,cjhp->cihp))/dot_general | solution.py:129
  274.9 3.2 reduce-window.19
  278.8 1.3 reduce-window.24
  280.1 1.3 slice_bitcast_fusion.2
  281.4 1.3 copy.68
  282.7 1.4 broadcast.255
  284.1 1.4 reshape.560
  285.5 3.0 fusion.36
  288.6 9.0 fusion.25
  297.9 1.2 fusion.55
  299.1 1.3 convolution_add_fusion.1
  300.9 1.3 copy-done.10
  302.1 0.7 copy-done.12
  302.9 2.4 multiply_reduce_fusion.4
  305.3 2.3 multiply_reduce_fusion.3
  307.6 1.0 slice_multiply_fusion.1
  308.6 1.0 slice_multiply_fusion
  309.6 1.0 slice_multiply_fusion.2
  310.6 1.8 fusion.75
  313.2 2.8 fusion.20
  316.0 6.6 copy.70
  323.4 31.1 %reduce-scatter.5.cloned.1.call-done = f32[8,1,64,4480]{3,2,0,1:T(8,128)} async-done(((f32[8,2,64,4480]{3,2,0,1:T(8,128)}), f32[8,1,64,4480]{3,2,0,1:T(8,128)}) %reduce-scatter.5.cloned.1.call-update) | async-done | bytes 9175056 | tf_op jit(solution)/shard_map/reduce_scatter | solution.py:156
  354.5 94.9 %reduce-scatter.11.cloned.1.call-done = f32[1,128,1024]{2,1,0:T(8,128)} async-done(((f32[8,128,1024]{2,1,0:T(8,128)}), f32[1,128,1024]{2,1,0:T(8,128)}) %reduce-scatter.11.cloned.1.call-update) | async-done | bytes 524304 | tf_op jit(solution)/shard_map/reduce_scatter | solution.py:157
  449.4 186.6 %reduce-scatter.7.cloned.1.call-done = f32[1,64,4480]{2,1,0:T(8,128)} async-done(((f32[8,64,4480]{2,1,0:T(8,128)}), f32[1,64,4480]{2,1,0:T(8,128)}) %reduce-scatter.7.cloned.1.call-update) | async-done | bytes 1146896 | tf_op jit(solution)/shard_map/reduce_scatter | solution.py:157
  637.0 1.4 copy.69
  638.4 2.0 reshape.564
  640.5 8.0 multiply_reduce_fusion.10
  648.5 0.7 concatenate.35
  649.2 76.7 %all-reduce.23.cloned.1.call-done = (f32[64,4480]{1,0:T(8,128)}, f32[128,1024]{1,0:T(8,128)}) async-done(((f32[64,4480]{1,0:T(8,128)}, f32[128,1024]{1,0:T(8,128)}), (f32[64,4480]{1,0:T(8,128)}, f32[128,1024]{1,0:T(8,128)})) %all-reduce.23.cloned.1.call-update) | async-done | bytes 1671184 | tf_op jit(solution)/shard_map/psum | solution.py:158
  726.6 2.9 fusion.39
  729.5 2.4 convolution_add_fusion
  731.9 311.2 %all-gather.26.cloned.1.call-done = f32[1024,1836]{1,0:T(8,128)} async-done(((f32[8,1836]{1,0:T(8,128)}), f32[1024,1836]{1,0:T(8,128)}) %all-gather.26.cloned.1.call-update) | async-done | bytes 7520272 | tf_op jit(solution)/shard_map/all_gather | solution.py:228
  1043.1 3.6 bitcast_reduce_fusion
  1047.6 0.7 copy.73
  1050.1 6.3 all-gather.16.cloned.1.call-done
  1056.4 16.4 %all-gather.14.cloned.1.call-done = f32[128,4480]{1,0:T(8,128)} async-done(((f32[64,4480]{1,0:T(8,128)}), f32[128,4480]{1,0:T(8,128)}) %all-gather.14.cloned.1.call-update) | async-done | bytes 2293776 | tf_op jit(solution)/shard_map/all_gather | solution.py:159
  1072.8 3.1 copy.72
  1075.9 1.0 copy.98
  (241 shorter events, 14.9 us)
Async XLA Ops:
  7.2 3.3 copy-start.29
  7.2 104.6 %all-gather.18.cloned.1.call-start = ((), (), s32[]{:S(2)}) async-start(), calls=%async_computation.10 | async-start | bytes 5160960 | tf_op jit(solution)/shard_map/all_gather | solution.py:147
  10.5 157.4 %all-gather.22.cloned.1.call-start = ((), (), s32[]{:S(2)}) async-start(), calls=%async_computation.12 | async-start | bytes 2359296 | tf_op jit(solution)/shard_map/all_gather | solution.py:147
  11.3 100.7 %copy-start.53 = (f32[288,4]{0,1:T(4,128)S(1)}, f32[288,4]{0,1:T(4,128)}, u32[]{:S(2)}) copy-start(f32[288,4]{0,1:T(4,128)} %param.17) | copy-start | bytes 13828
  11.3 182.1 %all-gather.20.cloned.1.call-start = ((), (), s32[]{:S(2)}) async-start(), calls=%async_computation.11 | async-start | bytes 13762560 | tf_op jit(solution)/shard_map/all_gather | solution.py:148
  111.8 29.2 %copy-start.70 = (s32[1,2]{1,0:T(1,128)S(1)}, s32[1,2]{1,0:T(1,128)}, u32[]{:S(2)}) copy-start(s32[1,2]{1,0:T(1,128)} %param.14) | copy-start | bytes 28
  111.9 31.2 %copy-start.11 = (f32[256,1024]{1,0:T(8,128)S(1)}, f32[256,1024]{1,0:T(8,128)}, u32[]{:S(2)}) copy-start(f32[256,1024]{1,0:T(8,128)} %param.12) | copy-start | bytes 3145732
  111.9 141.3 %all-gather.24.cloned.1.call-start = ((), (), s32[]{:S(2)}) async-start(), calls=%async_computation.13 | async-start | bytes 6291456 | tf_op jit(solution)/shard_map/all_gather | solution.py:148
  141.6 59.3 %copy-start.60 = (f32[32]{0:T(128)}, f32[32]{0:T(128)S(1)}, u32[]{:S(2)}) copy-start(f32[32]{0:T(128)S(1)} %neg.39) | copy-start | bytes 388
  141.7 59.2 %copy-start.62 = (f32[32]{0:T(128)}, f32[32]{0:T(128)S(1)}, u32[]{:S(2)}) copy-start(f32[32]{0:T(128)S(1)} %add.161) | copy-start | bytes 388
  145.4 67.1 %copy-start.31 = (f32[2304]{0:T(1024)}, f32[2304]{0:T(1024)S(1)}, u32[]{:S(2)}) copy-start(f32[2304]{0:T(1024)S(1)} %get-tuple-element.53) | copy-start | bytes 27652
  145.4 67.1 %copy-start.33 = (f32[2304]{0:T(1024)}, f32[2304]{0:T(1024)S(1)}, u32[]{:S(2)}) copy-start(f32[2304]{0:T(1024)S(1)} %get-tuple-element.54) | copy-start | bytes 27652
  145.4 67.1 %copy-start.35 = (f32[2304]{0:T(1024)}, f32[2304]{0:T(1024)S(1)}, u32[]{:S(2)}) copy-start(f32[2304]{0:T(1024)S(1)} %get-tuple-element.56) | copy-start | bytes 27652
  145.5 67.1 %copy-start.37 = (f32[2304]{0:T(1024)}, f32[2304]{0:T(1024)S(1)}, u32[]{:S(2)}) copy-start(f32[2304]{0:T(1024)S(1)} %get-tuple-element.55) | copy-start | bytes 27652
  145.5 47.9 %copy-start.44 = (f32[256]{0:T(256)}, f32[256]{0:T(256)S(1)}, u32[]{:S(2)}) copy-start(f32[256]{0:T(256)S(1)} %fusion.66) | copy-start | bytes 3076
  145.6 67.0 %copy-start.54 = (pred[256]{0:T(512)(128)(4,1)}, pred[256]{0:T(512)(128)(4,1)S(1)}, u32[]{:S(2)}) copy-start(pred[256]{0:T(512)(128)(4,1)S(1)} %get-tuple-element.90) | copy-start | bytes 772
  145.6 67.0 %copy-start.56 = (pred[256]{0:T(512)(128)(4,1)}, pred[256]{0:T(512)(128)(4,1)S(1)}, u32[]{:S(2)}) copy-start(pred[256]{0:T(512)(128)(4,1)S(1)} %get-tuple-element.91) | copy-start | bytes 772
  145.6 67.0 %copy-start.58 = (pred[256]{0:T(512)(128)(4,1)}, pred[256]{0:T(512)(128)(4,1)S(1)}, u32[]{:S(2)}) copy-start(pred[256]{0:T(512)(128)(4,1)S(1)} %get-tuple-element.92) | copy-start | bytes 772
  145.6 74.8 %copy-start.48 = (f32[256]{0:T(256)}, f32[256]{0:T(256)S(1)}, u32[]{:S(2)}) copy-start(f32[256]{0:T(256)S(1)} %get-tuple-element.89) | copy-start | bytes 3076
  167.9 154.8 %reduce-scatter.9.cloned.1.call-start = ((), (), s32[]{:S(2)}) async-start(), calls=%async_computation.7 | async-start | bytes 12582912 | tf_op jit(solution)/shard_map/reduce_scatter | solution.py:156
  204.6 4.7 copy-start.3
  220.2 13.7 %copy-start.21 = (f32[256,2048]{0,1:T(8,128)}, f32[256,2048]{0,1:T(8,128)S(1)}, u32[]{:S(2)}) copy-start(f32[256,2048]{0,1:T(8,128)S(1)} %slice.179) | copy-start | bytes 6291460
  220.2 4.5 copy-start.26
  220.3 4.5 copy-start.39
  220.5 13.5 %copy-start.42 = (f32[32,256]{1,0:T(8,128)}, f32[32,256]{1,0:T(8,128)S(1)}, u32[]{:S(2)}) copy-start(f32[32,256]{1,0:T(8,128)S(1)} %bitcast_add_fusion.2) | copy-start | bytes 98308
  221.5 12.4 %copy-start.24 = (f32[256,256]{1,0:T(8,128)}, f32[256,256]{1,0:T(8,128)S(1)}, u32[]{:S(2)}) copy-start(f32[256,256]{1,0:T(8,128)S(1)} %fusion.53) | copy-start | bytes 786436
  233.9 3.1 copy-start.15
  234.0 3.1 copy-start.19
  237.1 20.9 %copy-start.46 = (f32[256]{0:T(256)}, f32[256]{0:T(256)S(1)}, u32[]{:S(2)}) copy-start(f32[256]{0:T(256)S(1)} %fusion.67) | copy-start | bytes 3076
  252.4 102.0 %reduce-scatter.5.cloned.1.call-start = ((), (), s32[]{:S(2)}) async-start(), calls=%async_computation.4 | async-start | bytes 27525120 | tf_op jit(solution)/shard_map/reduce_scatter | solution.py:156
  253.2 4.8 copy-start.7
  253.2 4.8 copy-start.16
  258.0 4.2 copy-start.22
  258.0 4.2 copy-start.25
  258.0 4.1 copy-start.27
  258.1 4.1 copy-start.40
  258.1 4.1 copy-start.43
  262.2 11.4 %copy-start.4 = (f32[256,2048]{0,1:T(8,128)}, f32[256,2048]{0,1:T(8,128)S(1)}, u32[]{:S(2)}) copy-start(f32[256,2048]{0,1:T(8,128)S(1)} %get-tuple-element.60) | copy-start | bytes 6291460
  262.2 11.4 %copy-start.18 = (f32[256,32,64]{0,2,1:T(8,128)S(1)}, f32[256,32,64]{0,2,1:T(8,128)}, u32[]{:S(2)}) copy-start(f32[256,32,64]{0,2,1:T(8,128)} %copy-done.17) | copy-start | bytes 6291460
  285.5 12.1 %slice-start = ((s8[4489216]{0:T(1024)(128)(4,1)}), s8[4194304]{0:T(1024)(128)(4,1)S(1)}, s32[]{:S(2)}) async-start(s8[4489216]{0:T(1024)(128)(4,1)} %bitcast.137), calls=%async_computation.16 | async-start | bytes 8388608
  288.6 9.1 slice-start.1
  288.6 9.1 copy-start.28
  288.6 9.1 copy-start.30
  288.6 9.1 copy-start.61
  288.6 9.1 copy-start.63
  288.6 11.8 %copy-start.5 = (f32[256,2048]{0,1:T(8,128)S(1)}, f32[256,2048]{0,1:T(8,128)}, u32[]{:S(2)}) copy-start(f32[256,2048]{0,1:T(8,128)} %copy-done.4) | copy-start | bytes 6291460
  288.6 11.8 %copy-start.41 = (f32[2048]{0:T(1024)S(1)}, f32[2048]{0:T(1024)}, u32[]{:S(2)}) copy-start(f32[2048]{0:T(1024)} %mul.455) | copy-start | bytes 24580
  302.9 2.4 copy-start.8
  302.9 2.4 copy-start.9
  302.9 2.4 copy-start.55
  302.9 2.4 copy-start.57
  313.2 2.8 copy-start.13
  322.6 126.8 %reduce-scatter.11.cloned.1.call-start = ((), (), s32[]{:S(2)}) async-start(), calls=%async_computation.8 | async-start | bytes 4718592 | tf_op jit(solution)/shard_map/reduce_scatter | solution.py:157
  323.4 312.6 %reduce-scatter.7.cloned.1.call-start = ((), (), s32[]{:S(2)}) async-start(), calls=%async_computation.5 | async-start | bytes 10321920 | tf_op jit(solution)/shard_map/reduce_scatter | solution.py:157
  354.4 281.9 %copy-start.52 = (f32[2048]{0:T(1024)S(1)}, f32[2048]{0:T(1024)}, u32[]{:S(2)}) copy-start(f32[2048]{0:T(1024)} %get-tuple-element.47) | copy-start | bytes 24580
  354.5 371.5 %all-reduce.23.cloned.1.call-start = ((), (), s32[]{:S(2)}) async-start(), calls=%async_computation.15 | async-start | bytes 3342336 | tf_op jit(solution)/shard_map/psum | solution.py:158
  636.0 407.1 %all-gather.26.cloned.1.call-start = ((), (), s32[]{:S(2)}) async-start(), calls=%async_computation.14 | async-start | bytes 7925760 | tf_op jit(solution)/shard_map/all_gather | solution.py:228
  640.5 86.1 %copy-start.51 = (f32[256]{0:T(256)S(1)}, f32[256]{0:T(256)}, u32[]{:S(2)}) copy-start(f32[256]{0:T(256)} %copy-done.50) | copy-start | bytes 3076
  649.2 407.2 %all-gather.16.cloned.1.call-start = ((), (), s32[]{:S(2)}) async-start(), calls=%async_computation.9 | async-start | bytes 1572864 | tf_op jit(solution)/shard_map/all_gather | solution.py:159
  726.0 346.8 %all-gather.14.cloned.1.call-start = ((), (), s32[]{:S(2)}) async-start(), calls=%async_computation.6 | async-start | bytes 3440640 | tf_op jit(solution)/shard_map/all_gather | solution.py:159
  726.6 3.0 copy-start.47
  726.6 3.0 copy-start.20
  1056.4 19.5 %copy-start.23 = (f32[256,1024]{1,0:T(8,128)S(1)}, f32[256,1024]{1,0:T(8,128)}, u32[]{:S(2)}) copy-start(f32[256,1024]{1,0:T(8,128)} %all-gather.16.cloned.1.call-done) | copy-start | bytes 3145732
  1072.8 4.1 copy-start.1
  (22 other events, 35.6 us)
Sparse Core Ops, SparseCore 0:
  10.6 101.1 all-gather.17
  114.0 53.8 all-gather.21
  169.6 23.8 all-gather.19
  194.9 17.6 all-gather.23
  252.5 20.8 reduce-scatter.8
  322.7 31.6 reduce-scatter.4
  357.0 92.3 reduce-scatter.10
  451.9 183.9 reduce-scatter.6
  638.8 87.1 all-reduce.22
  728.1 314.9 all-gather.25
  1044.7 11.5 all-gather.15
  1057.9 14.8 all-gather.13
